TPU v7x, 32 devices: a whole 2x2x4 slice. The times are simulated.
32 devices in a mesh: seq: 4 (over y, x), fsdp: 8 (over z, core).
Axes of the slice: x: 2, y: 2, z: 4, core: 2. Of those that a mesh axis runs over, the one named last changes fastest.
Arguments:
- hidden_in: bfloat16 [8, 1024, 1024], P('fsdp', 'seq'), may hold values from -10 to 10
- segment_ids: int32 [8, 1024], P('fsdp'), may hold values from 0 to 2, never falling along the last dimension, each value on 1 to 768 neighbouring positions
- valid_tokens: int32 [8, 1024], P('fsdp'), may hold values from 0 to 1
- w_qkv: bfloat16 [1024, 3072], P('fsdp'), may hold values from -0.1875 to 0.1875
- w_attn_out: bfloat16 [1024, 1024], P('fsdp'), may hold values from -2 to 2
- w_in_proj: bfloat16 [1024, 5248], P('fsdp'), may hold values from -0.1875 to 0.1875
- w_out_proj: bfloat16 [2624, 1024], P('fsdp'), may hold values from -0.125 to 0.125
- attn_gain: bfloat16 [1024], P('fsdp'), may hold values from 0.25 to 1.75
- mlp_gain: bfloat16 [1024], P('fsdp'), may hold values from 0.25 to 1.75
- cotangent: bfloat16 [8, 1024, 1024], P('fsdp', 'seq'), may hold values from -6 to 6
Outputs:
- hidden_out: bfloat16 [8, 1024, 1024], P('fsdp', 'seq')
- grad_in: float32 [8, 1024, 1024], P('fsdp', 'seq')
- grad_qkv: float32 [1024, 3072], P('fsdp')
- grad_attn_out: float32 [1024, 1024], P('fsdp')
- grad_in_proj: float32 [1024, 5248], P('fsdp')
- grad_out_proj: float32 [2624, 1024], P('fsdp')
- grad_attn_gain: float32 [1024], P('fsdp')
- grad_mlp_gain: float32 [1024], P('fsdp')
- rms_values: float32 [3], replicated
All inputs are finite; a program needn't handle non-finite values.
Results may differ from a plain program's by a relative error of at most 0.014.
The roundings to bfloat16 on the way count: a program that leaves them out, or rounds other values in their place, can miss the bound.
Values may be sent and summed in bfloat16 or wider, within the bound.
No kernel may reach another device: no remote copies, remote signals or barrier semaphores. Data moves between devices by JAX's collectives and lax.ppermute only.
A program may use at most 192 MiB of HBM per device.

v0:
```python
import jax
import jax.numpy as jnp
from jax import lax
from jax.sharding import PartitionSpec as P

D = 1024
HEADS = 16
HD = 64
FF = 2624
ROPE_BASE = 160000.0
NORM_EPS = 1e-05


def norm_rows(values, gain_row):
    average = jnp.mean(values, axis=-1, keepdims=True)
    centered = values - average
    variance = jnp.mean(centered * centered, axis=-1, keepdims=True)
    return centered * lax.rsqrt(variance + NORM_EPS) * gain_row


def rotate(head_values, positions):
    half_width = head_values.shape[-1] // 2
    frequency = ROPE_BASE ** (
        -2.0 * jnp.arange(half_width, dtype=jnp.float32) / head_values.shape[-1]
    )
    angles = positions.astype(jnp.float32)[:, None] * frequency[None, :]
    cosine = jnp.cos(angles)[:, None, :]
    sine_part = jnp.sin(angles)[:, None, :]
    first_half = head_values[..., :half_width]
    second = head_values[..., half_width:]
    return jnp.concatenate(
        [first_half * cosine - second * sine_part, second * cosine + first_half * sine_part],
        axis=-1,
    )


def gelu_gate(inputs, gates):
    return 0.5 * inputs * (1.0 + jax.scipy.special.erf(inputs * 0.7071067811865476)) * gates


def allowed_mask(seg_block, row_ids, seg_all, valid_all):
    col_ids = jnp.arange(seg_all.shape[0], dtype=jnp.int32)
    return (seg_block[:, None] == seg_all[None, :]) & (
        (valid_all[None, :] > 0) | (row_ids[:, None] == col_ids[None, :])
    )


def attend_forward(queries, key_heads, value_heads, seg_all, valid_all):
    length, head_local, head_width = queries.shape
    block_rows = min(512, length)
    block_count = length // block_rows
    score_scale = float(head_width) ** (-0.5)
    row_ids = jnp.arange(length, dtype=jnp.int32).reshape(block_count, block_rows)

    def one_block(block_items):
        query_block, seg_block, row_block = block_items
        scores = (
            jnp.einsum("qhd,khd->hqk", query_block, key_heads, preferred_element_type=jnp.float32)
            * score_scale
        )
        allowed = allowed_mask(seg_block, row_block, seg_all, valid_all)[None]
        scores = jnp.where(allowed, scores, -1e30)
        row_max = jnp.max(scores, axis=-1, keepdims=True)
        exponent = jnp.exp(scores - row_max)
        denominator = jnp.sum(exponent, axis=-1, keepdims=True)
        weights = (exponent / denominator).astype(jnp.bfloat16)
        output = jnp.einsum(
            "hqk,khd->qhd", weights, value_heads, preferred_element_type=jnp.float32
        )
        return (output, (row_max + jnp.log(denominator))[..., 0])

    outputs, log_sums = lax.map(
        one_block,
        (
            queries.reshape(block_count, block_rows, head_local, head_width),
            seg_all.reshape(block_count, block_rows),
            row_ids,
        ),
    )
    return (outputs.reshape(length, head_local, head_width), log_sums)


def attend_backward(queries, key_heads, value_heads, grad_out, log_sums, seg_all, valid_all):
    length, head_local, head_width = queries.shape
    block_rows = min(512, length)
    block_count = length // block_rows
    score_scale = float(head_width) ** (-0.5)
    row_ids = jnp.arange(length, dtype=jnp.int32).reshape(block_count, block_rows)

    def one_block(carried, block_items):
        key_grad, value_grad = carried
        query_block, grad_block, lse_block, seg_block, row_block = block_items
        scores = (
            jnp.einsum("qhd,khd->hqk", query_block, key_heads, preferred_element_type=jnp.float32)
            * score_scale
        )
        allowed = allowed_mask(seg_block, row_block, seg_all, valid_all)[None]
        scores = jnp.where(allowed, scores, -1e30)
        weights = jnp.exp(scores - lse_block[..., None])
        weights_low = weights.astype(jnp.bfloat16)
        value_grad = value_grad + jnp.einsum(
            "hqk,qhd->khd", weights_low, grad_block, preferred_element_type=jnp.float32
        )
        weight_grad = jnp.einsum(
            "qhd,khd->hqk", grad_block, value_heads, preferred_element_type=jnp.float32
        )
        inner_sum = jnp.sum(weights * weight_grad, axis=-1, keepdims=True)
        score_grad = (weights * (weight_grad - inner_sum)).astype(jnp.bfloat16)
        query_grad = (
            jnp.einsum("hqk,khd->qhd", score_grad, key_heads, preferred_element_type=jnp.float32)
            * score_scale
        )
        key_grad = (
            key_grad
            + jnp.einsum(
                "hqk,qhd->khd", score_grad, query_block, preferred_element_type=jnp.float32
            )
            * score_scale
        )
        return ((key_grad, value_grad), query_grad)

    empty_grad = jnp.zeros((length, head_local, head_width), jnp.float32)
    block_items = (
        queries.reshape(block_count, block_rows, head_local, head_width),
        grad_out.reshape(block_count, block_rows, head_local, head_width),
        log_sums,
        seg_all.reshape(block_count, block_rows),
        row_ids,
    )
    (key_grad, value_grad), query_grads = lax.scan(one_block, (empty_grad, empty_grad), block_items)
    return (query_grads.reshape(length, head_local, head_width), key_grad, value_grad)


def on_device(
    hidden_in,
    segment_ids,
    valid_tokens,
    w_qkv,
    w_attn_out,
    w_in_proj,
    w_out_proj,
    attn_gain,
    mlp_gain,
    cotangent,
):
    seq_size = lax.axis_size("seq")
    seq_index = lax.axis_index("seq")
    inputs = hidden_in[0].astype(jnp.float32)
    tokens = inputs.shape[0]
    length = tokens * seq_size
    head_local = HEADS // seq_size
    seg_all = segment_ids[0]
    valid_all = valid_tokens[0]
    offset = seq_index * tokens
    valid_mine = lax.dynamic_slice_in_dim(valid_all, offset, tokens).astype(jnp.float32)[:, None]
    positions = offset + jnp.arange(tokens, dtype=jnp.int32)
    attn_full = (
        lax.all_gather(w_qkv, "fsdp", axis=0, tiled=True),
        lax.all_gather(w_attn_out, "fsdp", axis=0, tiled=True),
        lax.all_gather(attn_gain, "fsdp", axis=0, tiled=True),
    )
    mlp_full = (
        lax.all_gather(w_in_proj, "fsdp", axis=0, tiled=True),
        lax.all_gather(w_out_proj, "fsdp", axis=0, tiled=True),
        lax.all_gather(mlp_gain, "fsdp", axis=0, tiled=True),
    )
    qkv_weight, out_weight, gain_one = attn_full
    in_weight, down_weight, gain_two = mlp_full
    gain_one = gain_one.astype(jnp.float32)
    gain_two = gain_two.astype(jnp.float32)
    normed_low = norm_rows(inputs, gain_one).astype(jnp.bfloat16)
    projected = jnp.dot(normed_low, qkv_weight, preferred_element_type=jnp.float32).reshape(
        tokens, 3, HEADS, HD
    )

    def rope_pair(pair_heads):
        return jnp.stack(
            [rotate(pair_heads[:, 0], positions), rotate(pair_heads[:, 1], positions)], axis=1
        )

    turned = jnp.concatenate([rope_pair(projected[:, :2]), projected[:, 2:]], axis=1).astype(
        jnp.bfloat16
    )
    by_heads = lax.all_to_all(
        turned.reshape(tokens, 3, seq_size, head_local * HD),
        "seq",
        split_axis=2,
        concat_axis=0,
        tiled=True,
    )
    by_heads = by_heads.reshape(length, 3, head_local, HD)
    queries = by_heads[:, 0]
    key_heads = by_heads[:, 1]
    value_heads = by_heads[:, 2]
    attended, log_sums = attend_forward(queries, key_heads, value_heads, seg_all, valid_all)
    attended_low = attended.astype(jnp.bfloat16).reshape(length, 1, head_local * HD)
    mixed_low = lax.all_to_all(
        attended_low, "seq", split_axis=0, concat_axis=1, tiled=True
    ).reshape(tokens, D)
    attn_branch = jnp.dot(mixed_low, out_weight, preferred_element_type=jnp.float32)
    middle = inputs + attn_branch
    normed_two_low = norm_rows(middle, gain_two).astype(jnp.bfloat16)
    widened = jnp.dot(normed_two_low, in_weight, preferred_element_type=jnp.float32)
    inner_in = widened[:, :FF]
    inner_gate = widened[:, FF:]
    hidden_low = gelu_gate(inner_in, inner_gate).astype(jnp.bfloat16)
    mlp_branch = jnp.dot(hidden_low, down_weight, preferred_element_type=jnp.float32)
    result = middle + mlp_branch
    stat_sums = lax.psum(
        (
            jnp.sum(valid_mine * result * result),
            jnp.sum(valid_mine * attn_branch * attn_branch),
            jnp.sum(valid_mine * mlp_branch * mlp_branch),
            jnp.sum(valid_mine),
        ),
        ("seq", "fsdp"),
    )
    valid_count = jnp.maximum(stat_sums[3], 1.0)
    root_means = jnp.sqrt(jnp.stack([stat_sums[0], stat_sums[1], stat_sums[2]]) / (valid_count * D))
    back_attn = (
        lax.all_gather(w_qkv, "fsdp", axis=0, tiled=True),
        lax.all_gather(w_attn_out, "fsdp", axis=0, tiled=True),
        lax.all_gather(attn_gain, "fsdp", axis=0, tiled=True),
    )
    back_mlp = (
        lax.all_gather(w_in_proj, "fsdp", axis=0, tiled=True),
        lax.all_gather(w_out_proj, "fsdp", axis=0, tiled=True),
        lax.all_gather(mlp_gain, "fsdp", axis=0, tiled=True),
    )
    qkv_back, out_back = (back_attn[0], back_attn[1])
    in_back, down_back = (back_mlp[0], back_mlp[1])
    grad_result = cotangent[0].astype(jnp.float32)
    grad_mlp_low = grad_result.astype(jnp.bfloat16)
    grad_down = jnp.einsum(
        "tf,td->fd", hidden_low, grad_mlp_low, preferred_element_type=jnp.float32
    )
    grad_hidden = jnp.einsum(
        "td,fd->tf", grad_mlp_low, down_back, preferred_element_type=jnp.float32
    )
    _, gelu_pull = jax.vjp(gelu_gate, inner_in, inner_gate)
    grad_inner_in, grad_inner_gate = gelu_pull(grad_hidden)
    grad_widened = jnp.concatenate([grad_inner_in, grad_inner_gate], axis=1).astype(jnp.bfloat16)
    grad_in_weight = jnp.einsum(
        "td,tf->df", normed_two_low, grad_widened, preferred_element_type=jnp.float32
    )
    grad_normed_two = jnp.einsum(
        "tf,df->td", grad_widened, in_back, preferred_element_type=jnp.float32
    )
    _, second_pull = jax.vjp(norm_rows, middle, gain_two)
    grad_middle_part, grad_gain_two = second_pull(grad_normed_two)
    grad_middle = grad_result + grad_middle_part
    mlp_sums = (
        lax.psum_scatter(grad_in_weight, "fsdp", scatter_dimension=0, tiled=True),
        lax.psum_scatter(grad_down, "fsdp", scatter_dimension=0, tiled=True),
        lax.psum_scatter(grad_gain_two, "fsdp", scatter_dimension=0, tiled=True),
    )
    grad_attn_low = grad_middle.astype(jnp.bfloat16)
    grad_out_weight = jnp.einsum(
        "td,te->de", mixed_low, grad_attn_low, preferred_element_type=jnp.float32
    )
    grad_mixed = jnp.einsum(
        "te,de->td", grad_attn_low, out_back, preferred_element_type=jnp.float32
    ).astype(jnp.bfloat16)
    grad_by_heads = lax.all_to_all(
        grad_mixed.reshape(tokens, seq_size, head_local * HD),
        "seq",
        split_axis=1,
        concat_axis=0,
        tiled=True,
    )
    grad_by_heads = grad_by_heads.reshape(length, head_local, HD)
    query_grad, key_grad, value_grad = attend_backward(
        queries, key_heads, value_heads, grad_by_heads, log_sums, seg_all, valid_all
    )
    stacked = (
        jnp.stack([query_grad, key_grad, value_grad], axis=1)
        .astype(jnp.bfloat16)
        .reshape(length, 3, 1, head_local * HD)
    )
    grad_turned = (
        lax.all_to_all(stacked, "seq", split_axis=0, concat_axis=2, tiled=True)
        .reshape(tokens, 3, HEADS, HD)
        .astype(jnp.float32)
    )
    _, rope_pull = jax.vjp(rope_pair, projected[:, :2])
    (grad_pair,) = rope_pull(grad_turned[:, :2])
    grad_projected = (
        jnp.concatenate([grad_pair, grad_turned[:, 2:]], axis=1)
        .reshape(tokens, 3 * D)
        .astype(jnp.bfloat16)
    )
    grad_qkv_weight = jnp.einsum(
        "td,te->de", normed_low, grad_projected, preferred_element_type=jnp.float32
    )
    grad_normed = jnp.einsum(
        "te,de->td", grad_projected, qkv_back, preferred_element_type=jnp.float32
    )
    _, first_pull = jax.vjp(norm_rows, inputs, gain_one)
    grad_input_part, grad_gain_one = first_pull(grad_normed)
    grad_inputs = grad_middle + grad_input_part
    attn_sums = (
        lax.psum_scatter(grad_qkv_weight, "fsdp", scatter_dimension=0, tiled=True),
        lax.psum_scatter(grad_out_weight, "fsdp", scatter_dimension=0, tiled=True),
        lax.psum_scatter(grad_gain_one, "fsdp", scatter_dimension=0, tiled=True),
    )
    summed = lax.psum(
        (attn_sums[0], attn_sums[1], attn_sums[2], mlp_sums[0], mlp_sums[1], mlp_sums[2]), "seq"
    )
    final_grads = (summed[0], summed[1], summed[3], summed[4], summed[2], summed[5])
    return (
        result.astype(jnp.bfloat16)[None],
        grad_inputs[None],
        final_grads[0],
        final_grads[1],
        final_grads[2],
        final_grads[3],
        final_grads[4],
        final_grads[5],
        root_means,
    )


def solution(mesh):
    in_specs = (
        P("fsdp", "seq", None),
        P("fsdp", None),
        P("fsdp", None),
        P("fsdp", None),
        P("fsdp", None),
        P("fsdp", None),
        P("fsdp", None),
        P("fsdp"),
        P("fsdp"),
        P("fsdp", "seq", None),
    )
    out_specs = (
        P("fsdp", "seq", None),
        P("fsdp", "seq", None),
        P("fsdp", None),
        P("fsdp", None),
        P("fsdp", None),
        P("fsdp", None),
        P("fsdp"),
        P("fsdp"),
        P(),
    )
    return jax.shard_map(
        on_device, mesh=mesh, in_specs=in_specs, out_specs=out_specs, check_vma=False
    )
```

profile of v0, /device:TPU:0, one launch (start us, length us, event | category | flops | bytes accessed | tf_op | source)
XLA Modules:
  0.0 950.7 jit_solution(4761089183071408924)
XLA Ops:
  9.4 13.6 %all-gather = bf16[8,1,128]{2,1,0:T(2,128)(2,1)S(1)} all-gather(bf16[1,1,128]{2,1,0:T(2,128)(2,1)} %bitcast.267), channel_id=1, replica_groups=mesh['seq'=4,'fsdp'=8] {'fsdp'}, dimensions={0}, use_global_device_ids=true | all-gather | bytes 2304 | tf_op jit(solution)/shard_map/all_gather | solution.py:160
  24.8 52.3 %all-gather.7.cloned.1.call-done = bf16[1024,3072]{1,0:T(8,128)(2,1)} async-done(((bf16[128,3072]{1,0:T(8,128)(2,1)}), bf16[1024,3072]{1,0:T(8,128)(2,1)}) %all-gather.7.cloned.1.call-update) | async-done | bytes 6291472 | tf_op jit(solution)/shard_map/all_gather | solution.py:158
  77.1 8.7 copy.74
  98.1 18.0 %all-to-all-done = bf16[256,3,4,256]{0,3,1,2:T(8,128)(2,1)S(1)} async-done(((bf16[256,3,4,256]{0,3,1,2:T(8,128)(2,1)}), bf16[256,3,4,256]{0,3,1,2:T(8,128)(2,1)S(1)}, u32[]{:S(2)}, u32[]{:S(2)}) %all-to-all-start) | async-done | bytes 1572896 | tf_op jit(solution)/shard_map/all_to_all | solution.py:184
  124.5 15.6 %while.27 = (s32[]{:T(128)}, bf16[2,512,4,64]{1,3,2,0:T(8,128)(2,1)S(1)}, f32[2,4,512]{2,1,0:T(4,128)S(1)}, s32[2,512]{1,0:T(2,128)S(1)}, s32[1,1024]{1,0:T(1,12...) while((s32[]{:T(128)}, ...), condition=%wide.region_5.6_spmd, body=%wide.region_2.5_spmd.sunk | while | flops 564132864 | bytes 29186172 | solution.py:72
  156.8 10.5 %all-gather.1 = bf16[8,1,128]{2,1,0:T(2,128)(2,1)S(1)} all-gather(bf16[1,1,128]{2,1,0:T(2,128)(2,1)S(1)} %bitcast.268), channel_id=1, replica_groups=mesh['seq'=4,'fsdp'=8] {'fsdp'}, dimensions={0}, use_global_device_ids=true | all-gather | bytes 2304 | tf_op jit(solution)/shard_map/all_gather | solution.py:165
  176.8 32.4 %all-gather.11.cloned.1.call-done = bf16[1024,5248]{1,0:T(8,128)(2,1)} async-done(((bf16[128,5248]{1,0:T(8,128)(2,1)}), bf16[1024,5248]{1,0:T(8,128)(2,1)}) %all-gather.11.cloned.1.call-update) | async-done | bytes 10747920 | tf_op jit(solution)/shard_map/all_gather | solution.py:163
  209.2 9.0 fusion.81
  218.2 47.9 %all-gather.13.cloned.1.call-done = bf16[2624,1024]{1,0:T(8,128)(2,1)} async-done(((bf16[328,1024]{1,0:T(8,128)(2,1)}), bf16[2624,1024]{1,0:T(8,128)(2,1)}) %all-gather.13.cloned.1.call-update) | async-done | bytes 5373968 | tf_op jit(solution)/shard_map/all_gather | solution.py:164
  266.1 9.1 add_convert_fusion
  281.5 6.7 fusion.61
  293.7 7.0 fusion.67
  307.9 8.3 all-to-all-done.2
  321.0 42.2 %while.28 = (s32[]{:T(128)}, f32[1024,4,64]{0,2,1:T(8,128)S(1)}, f32[1024,4,64]{0,2,1:T(8,128)}, bf16[2,512,4,64]{1,3,2,0:T(8,128)(2,1)}, bf16[2,512,4,64]{1,3,2...) while((s32[]{:T(128)}, f32[1024,4,64]{0,2,1:T(8,128)S(1)}, ...), condition=%wide.region_12.13_spmd.clone, body=%wide.region_10.12_spmd.clone.sunk | while | flops 1377172480 | bytes 143735600 | solution.py:130
  370.8 28.0 %all_to_all.54 = bf16[1024,3,1,256]{3,1,2,0:T(4,128)(2,1)S(1)} all-to-all(bf16[1024,3,1,256]{3,1,2,0:T(4,128)(2,1)S(1)} %copy.90), channel_id=1, replica_groups=mesh['seq'=4,'fsdp'=8] {'seq'}, dimensions={0} | all-to-all | bytes 3145728 | tf_op jit(solution)/shard_map/all_to_all | solution.py:281
  406.4 6.6 fusion.71
  414.2 11.0 %fusion.46 = f32[1024,5248]{1,0:T(8,128)} fusion(bf16[256,2624]{1,0:T(8,128)(2,1)} %get-tuple-element.352, bf16[256,2624]{1,0:T(8,128)(2,1)} %get-tuple-element.351, f32[256,1024]{1,0:T(8,128)S(1)} %copy-done.3, f32[1024]{0:T(1024)S(1)} %bitcast.254, f32[256]{0:T(256)S(1)} %fusion.74, f32[256]{0:T(256)S(1)} %broadcast_multiply_fusion), kind=kOutput, calls=%fused_computation.69 | convolution fusion | flops 2757885952 | bytes 25237504 | tf_op jit(solution)/shard_map/td,tf->df/dot_general | solution.py:243
  425.3 28.7 %reduce-scatter.11.cloned.1.call-done = f32[328,1024]{1,0:T(8,128)} async-done(((f32[2624,1024]{1,0:T(8,128)}), f32[328,1024]{1,0:T(8,128)}) %reduce-scatter.11.cloned.1.call-update) | async-done | bytes 1343504 | tf_op jit(solution)/shard_map/reduce_scatter | solution.py:254
  454.0 129.9 %reduce-scatter.5.cloned.1.call-done = f32[128,3072]{1,0:T(8,128)} async-done(((f32[1024,3072]{1,0:T(8,128)}), f32[128,3072]{1,0:T(8,128)}) %reduce-scatter.5.cloned.1.call-update) | async-done | bytes 1572880 | tf_op jit(solution)/shard_map/reduce_scatter | solution.py:302
  583.9 213.4 %reduce-scatter.9.cloned.1.call-done = f32[128,5248]{1,0:T(8,128)} async-done(((f32[1024,5248]{1,0:T(8,128)}), f32[128,5248]{1,0:T(8,128)}) %reduce-scatter.9.cloned.1.call-update) | async-done | bytes 2686992 | tf_op jit(solution)/shard_map/reduce_scatter | solution.py:253
  798.6 39.2 %all-reduce.8 = (f32[1]{0:T(128)}, f32[1]{0:T(128)}, f32[1]{0:T(128)}, f32[]{:T(128)}) all-reduce(f32[1]{0:T(128)} %bitcast.50, f32[1]{0:T(128)} %bitcast.49, f32[1]{0:T(128)} %bitcast.48, f32[]{:T(128)} %get-tuple-element.337), channel_id=1, replica_groups=mesh['seq'=4,'fsdp'=8] {'seq','fsdp'}, use_global_device_ids=true, to_apply=%region_34.35 | all-reduce | flops 4 | bytes 32 | tf_op jit(solution)/shard_map/psum | solution.py:209
  847.5 16.0 %all-reduce.9 = (f32[1024]{0:T(1024)S(1)}, f32[1024]{0:T(1024)S(1)}) all-reduce(f32[1024]{0:T(1024)S(1)} %get-tuple-element.272, f32[1024]{0:T(1024)S(1)} %copy-done.36), channel_id=6, replica_groups=mesh['seq'=4,'fsdp'=8] {'fsdp'}, use_global_device_ids=true, to_apply=%region_24.25.clone | all-reduce | flops 2048 | bytes 16384
  863.6 9.2 all-reduce.10
  875.7 60.8 %all-reduce.14.cloned.1.call-done = (f32[128,3072]{1,0:T(8,128)}, f32[128,1024]{1,0:T(8,128)}, f32[128,5248]{1,0:T(8,128)}, f32[328,1024]{1,0:T(8,128)}) async-done(((f32[128,3072]{1,0:T(8,128)}, f32[128,1024]{1,0:T(8,128)}, f32[128,5248]{1,0:T(8,128)}, f32[328,1024]{1,0:T(8,128)}), (f32[128,3072]{1,0:T(8,128)}, f32[128,1024]{1,0:T(8,128)}, f32[128,5248]{1,0:T(8,128)}, ...) | async-done | bytes 6127632 | tf_op jit(solution)/shard_map/psum | solution.py:306
  (226 shorter events, 168.3 us)
Async XLA Ops:
  7.2 17.1 %copy-start.4 = (bf16[1,256,1024]{2,1,0:T(8,128)(2,1)S(1)}, bf16[1,256,1024]{2,1,0:T(8,128)(2,1)}, u32[]{:S(2)}) copy-start(bf16[1,256,1024]{2,1,0:T(8,128)(2,1)} %param.14) | copy-start | bytes 1572868
  7.2 69.9 %all-gather.7.cloned.1.call-start = ((), (), s32[]{:S(2)}) async-start(), calls=%async_computation.8 | async-start | bytes 7077888 | tf_op jit(solution)/shard_map/all_gather | solution.py:158
  7.9 165.1 %all-gather.9.cloned.1.call-start = ((), (), s32[]{:S(2)}) async-start(), calls=%async_computation.9 | async-start | bytes 2359296 | tf_op jit(solution)/shard_map/all_gather | solution.py:159
  8.7 200.5 %all-gather.11.cloned.1.call-start = ((), (), s32[]{:S(2)}) async-start(), calls=%async_computation.10 | async-start | bytes 12091392 | tf_op jit(solution)/shard_map/all_gather | solution.py:163
  23.0 62.7 %copy-start.26 = (f32[8,1,128]{2,1,0:T(1,128)}, f32[8,1,128]{2,1,0:T(1,128)S(1)}, u32[]{:S(2)}) copy-start(f32[8,1,128]{2,1,0:T(1,128)S(1)} %convert_element_type.149) | copy-start | bytes 12292
  24.3 61.5 %copy-start.28 = (f32[256]{0:T(256)}, f32[256]{0:T(256)S(1)}, u32[]{:S(2)}) copy-start(f32[256]{0:T(256)S(1)} %broadcast_multiply_fusion.1) | copy-start | bytes 3076
  24.6 61.2 %copy-start.34 = (f32[256]{0:T(256)}, f32[256]{0:T(256)S(1)}, u32[]{:S(2)}) copy-start(f32[256]{0:T(256)S(1)} %fusion.54) | copy-start | bytes 3076
  24.6 61.2 %copy-start.30 = (f32[256]{0:T(256)}, f32[256]{0:T(256)S(1)}, u32[]{:S(2)}) copy-start(f32[256]{0:T(256)S(1)} %fusion.73) | copy-start | bytes 3076
  24.8 66.1 %copy-start.22 = (f32[256,32]{0,1:T(8,128)}, f32[256,32]{0,1:T(8,128)S(1)}, u32[]{:S(2)}) copy-start(f32[256,32]{0,1:T(8,128)S(1)} %get-tuple-element.374) | copy-start | bytes 98308
  24.8 66.1 %copy-start.24 = (f32[256,32]{0,1:T(8,128)}, f32[256,32]{0,1:T(8,128)S(1)}, u32[]{:S(2)}) copy-start(f32[256,32]{0,1:T(8,128)S(1)} %get-tuple-element.375) | copy-start | bytes 98308
  92.7 23.5 %all-to-all-start = ((bf16[256,3,4,256]{0,3,1,2:T(8,128)(2,1)}), bf16[256,3,4,256]{0,3,1,2:T(8,128)(2,1)S(1)}, u32[]{:S(2)}, u32[]{:S(2)}) async-start(bf16[256,3,4,256]{0,3,1,2:T(8,128)(2,1)} %pad_maximum_fusion.3), calls=%async_computation | async-start | bytes 3145728 | tf_op jit(solution)/shard_map/all_to_all | solution.py:184
  96.4 169.7 %all-gather.13.cloned.1.call-start = ((), (), s32[]{:S(2)}) async-start(), calls=%async_computation.11 | async-start | bytes 6045696 | tf_op jit(solution)/shard_map/all_gather | solution.py:164
  152.6 15.3 %all-to-all-start.1 = ((bf16[4,2,32768]{2,1,0:T(2,128)(2,1)}), bf16[4,2,32768]{2,1,0:T(2,128)(2,1)}, u32[]{:S(2)}, u32[]{:S(2)}) async-start(bf16[4,2,32768]{2,1,0:T(2,128)(2,1)} %reshape.507), calls=%async_computation.1 | async-start | bytes 1048576 | tf_op jit(solution)/shard_map/all_to_all | solution.py:197
  156.7 268.6 %reduce-scatter.7.cloned.1.call-start = ((), (), s32[]{:S(2)}) async-start(), calls=%async_computation.13 | async-start | bytes 4718592 | tf_op jit(solution)/shard_map/reduce_scatter | solution.py:303
  176.5 111.7 %copy-start.2 = (f32[256,1024]{1,0:T(8,128)}, f32[256,1024]{1,0:T(8,128)S(1)}, u32[]{:S(2)}) copy-start(f32[256,1024]{1,0:T(8,128)S(1)} %get-tuple-element.342) | copy-start | bytes 3145732
  209.2 56.9 %copy-start.12 = (bf16[1,256,1024]{2,1,0:T(8,128)(2,1)S(1)}, bf16[1,256,1024]{2,1,0:T(8,128)(2,1)}, u32[]{:S(2)}) copy-start(bf16[1,256,1024]{2,1,0:T(8,128)(2,1)} %param.23) | copy-start | bytes 1572868
  292.7 161.3 %reduce-scatter.11.cloned.1.call-start = ((), (), s32[]{:S(2)}) async-start(), calls=%async_computation.15 | async-start | bytes 12091392 | tf_op jit(solution)/shard_map/reduce_scatter | solution.py:254
  304.0 12.2 %all-to-all-start.2 = ((bf16[256,4,256]{0,2,1:T(8,128)(2,1)}), bf16[256,4,256]{0,2,1:T(8,128)(2,1)S(1)}, u32[]{:S(2)}, u32[]{:S(2)}) async-start(bf16[256,4,256]{0,2,1:T(8,128)(2,1)} %bitcast.33), calls=%async_computation.2 | async-start | bytes 1048576 | tf_op jit(solution)/shard_map/all_to_all | solution.py:264
  307.7 276.2 %reduce-scatter.5.cloned.1.call-start = ((), (), s32[]{:S(2)}) async-start(), calls=%async_computation.12 | async-start | bytes 14155776 | tf_op jit(solution)/shard_map/reduce_scatter | solution.py:302
  413.0 384.3 %reduce-scatter.9.cloned.1.call-start = ((), (), s32[]{:S(2)}) async-start(), calls=%async_computation.14 | async-start | bytes 24182784 | tf_op jit(solution)/shard_map/reduce_scatter | solution.py:253
  425.2 372.1 %copy-start.38 = (u32[32]{0:T(128)S(1)}, u32[32]{0:T(128)}, u32[]{:S(2)}) copy-start(u32[32]{0:T(128)} %constant.113) | copy-start | bytes 388
  425.2 511.3 %all-reduce.14.cloned.1.call-start = ((), (), s32[]{:S(2)}) async-start(), calls=%async_computation.16 | async-start | bytes 12255232 | tf_op jit(solution)/shard_map/psum | solution.py:306
  841.0 31.9 %copy-start.8 = (f32[256,1024]{1,0:T(8,128)S(1)}, f32[256,1024]{1,0:T(8,128)}, u32[]{:S(2)}) copy-start(f32[256,1024]{1,0:T(8,128)} %copy-done.7) | copy-start | bytes 3145732
  841.0 31.9 %copy-start.33 = (f32[256]{0:T(256)S(1)}, f32[256]{0:T(256)}, u32[]{:S(2)}) copy-start(f32[256]{0:T(256)} %copy-done.32) | copy-start | bytes 3076
  (31 other events, 121.7 us)
Sparse Core Ops, SparseCore 0:
  9.6 67.4 all-gather.6
  78.7 27.8 all-gather.8
  108.2 100.9 all-gather.10
  210.7 55.3 all-gather.12
  292.8 48.6 reduce-scatter.6
  343.7 110.2 reduce-scatter.10
  456.3 127.5 reduce-scatter.4
  586.3 210.9 reduce-scatter.8
  801.2 135.2 all-reduce.13
where the time goes:
time: 956 us; the launch traced here: 951 us
  waiting for transfers between devices  594 us (62%)
  matrix products  117 us (12%)
  blocking collectives  116 us (12%)
  local copies, waits for them, and re-layouts  60.1 us (6%)
  other arithmetic  34.9 us (4%)
  between operations  16 us (2%)
  starting transfers between devices  12.1 us (1%)
    reduce_scatter x1, waiting for transfers between devices, on_device(): lax.psum_scatter(grad_in_weight, 'fsdp', scatter_dimension=0, tiled=True)  213 us
    reduce_scatter x1, waiting for transfers between devices, on_device(): lax.psum_scatter(grad_qkv_weight, 'fsdp', scatter_dimension=0, tiled=True)  130 us
    psum x1, waiting for transfers between devices, on_device(): lax.psum((attn_sums[0], attn_sums[1], attn_sums[2], mlp_sums[0], mlp_sums...  60.8 us
    all_gather x1, waiting for transfers between devices, on_device(): lax.all_gather(w_qkv, 'fsdp', axis=0, tiled=True)  52.3 us
    all_gather x1, waiting for transfers between devices, on_device(): lax.all_gather(w_out_proj, 'fsdp', axis=0, tiled=True)  47.9 us
    psum x1, blocking collectives, on_device(): lax.psum((jnp.sum(valid_mine * result * result), jnp.sum(valid_mine * att...  39.2 us
    all_gather x1, waiting for transfers between devices, on_device(): lax.all_gather(w_in_proj, 'fsdp', axis=0, tiled=True)  32.4 us
    reduce_scatter x1, waiting for transfers between devices, on_device(): lax.psum_scatter(grad_down, 'fsdp', scatter_dimension=0, tiled=True)  28.7 us
  transfers between devices with their start and end apart: 12, of which 9 were waited for; matrix products, arithmetic and copies ran while one was open for 18% of the time, Pallas kernels for 0%

commit v1 on v0

--- a/solution.py
+++ b/solution.py
@@ -1,3 +1,4 @@
+import functools
 import jax
 import jax.numpy as jnp
 from jax import lax
@@ -9,6 +10,24 @@
 FF = 2624
 ROPE_BASE = 160000.0
 NORM_EPS = 1e-05
+
+
+def _name_stacks_all(buf, a_name):
+    raw_out = lax.axis_size(a_name)
+    ready = lax.axis_index(a_name)
+    seen_now, even = (raw_out, ready)
+    moved, all_rows = (buf, 1)
+    while all_rows < seen_now:
+        small = map(lambda dev_j: (dev_j, dev_j ^ all_rows), range(seen_now))
+        finding = lax.ppermute(moved, a_name, list(small))
+        field_out = jnp.concatenate([moved, finding], axis=0)
+        met_up = jnp.concatenate([finding, moved], axis=0)
+        moved = jnp.where(even & all_rows == 0, field_out, met_up)
+        all_rows = 2 * all_rows
+    return moved
+
+
+search_the_object = functools.partial(_name_stacks_all, a_name="fsdp")
 
 
 def norm_rows(values, gain_row):
@@ -160,7 +179,7 @@
         lax.all_gather(attn_gain, "fsdp", axis=0, tiled=True),
     )
     mlp_full = (
-        lax.all_gather(w_in_proj, "fsdp", axis=0, tiled=True),
+        search_the_object(w_in_proj),
         lax.all_gather(w_out_proj, "fsdp", axis=0, tiled=True),
         lax.all_gather(mlp_gain, "fsdp", axis=0, tiled=True),
     )

time: 956 us -> 1220 us (1.28)
  waiting for transfers between devices: 594 us -> 750 us
  blocking collectives: 116 us -> 209 us
    ppermute x0 -> x3, waiting for transfers between devices: none -> 205 us  [_name_stacks_all(): finding = lax.ppermute(moved, a_name, list(small))]
    all_gather x1, blocking collectives: 10.5 us -> 104 us  [on_device(): lax.all_gather(mlp_gain, 'fsdp', axis=0, tiled=True)]
    all_gather x1, waiting for transfers between devices: 47.9 us -> 0.01 us  [on_device(): lax.all_gather(w_out_proj, 'fsdp', axis=0, tiled=True)]
    all_gather x1, waiting for transfers between devices: 52.3 us -> 87.9 us  [on_device(): lax.all_gather(w_qkv, 'fsdp', axis=0, tiled=True)]
    all_gather x1, waiting for transfers between devices: 32.4 us -> 0.01 us  [on_device(): lax.all_gather(w_in_proj, 'fsdp', axis=0, tiled=True)]
    all_to_all x1, waiting for transfers between devices: 18 us -> 1.3 us  [on_device(): lax.all_to_all(turned.reshape(tokens, 3, seq_size, head_local * HD), 'seq...]
    reduce_scatter x1, waiting for transfers between devices: 28.7 us -> 42.1 us  [on_device(): lax.psum_scatter(grad_down, 'fsdp', scatter_dimension=0, tiled=True)]
  transfers between devices with their start and end apart: 12 -> 15, of which waited for: 9 -> 8; matrix products, arithmetic and copies ran while one was open for 18% -> 16% of each run, Pallas kernels for 0% -> 0%
where the time goes in v1:
time: 1220 us
  waiting for transfers between devices  750 us (61%)
  blocking collectives  209 us (17%)
  matrix products  116 us (10%)
  local copies, waits for them, and re-layouts  60.3 us (5%)
  other arithmetic  44.6 us (4%)
  starting transfers between devices  22 us (2%)
  between operations  16 us (1%)
    reduce_scatter x1, waiting for transfers between devices, on_device(): lax.psum_scatter(grad_in_weight, 'fsdp', scatter_dimension=0, tiled=True)  213 us
    ppermute x3, waiting for transfers between devices, _name_stacks_all(): finding = lax.ppermute(moved, a_name, list(small))  205 us
    reduce_scatter x1, waiting for transfers between devices, on_device(): lax.psum_scatter(grad_qkv_weight, 'fsdp', scatter_dimension=0, tiled=True)  130 us
    all_gather x1, blocking collectives, on_device(): lax.all_gather(mlp_gain, 'fsdp', axis=0, tiled=True)  104 us
    all_gather x1, waiting for transfers between devices, on_device(): lax.all_gather(w_qkv, 'fsdp', axis=0, tiled=True)  87.9 us
    psum x1, waiting for transfers between devices, on_device(): lax.psum((attn_sums[0], attn_sums[1], attn_sums[2], mlp_sums[0], mlp_sums...  60.8 us
    reduce_scatter x1, waiting for transfers between devices, on_device(): lax.psum_scatter(grad_down, 'fsdp', scatter_dimension=0, tiled=True)  42.1 us
    psum x1, blocking collectives, on_device(): lax.psum((jnp.sum(valid_mine * result * result), jnp.sum(valid_mine * att...  39.2 us
  transfers between devices with their start and end apart: 15, of which 8 were waited for; matrix products, arithmetic and copies ran while one was open for 16% of the time, Pallas kernels for 0%

profile of v1, /device:TPU:0, one launch (start us, length us, event | category | flops | bytes accessed | tf_op | source)
XLA Modules:
  0.0 1218.8 jit_solution(4594216629439415807)
XLA Ops:
  10.6 13.2 %all-gather = bf16[8,1,128]{2,1,0:T(2,128)(2,1)S(1)} all-gather(bf16[1,1,128]{2,1,0:T(2,128)(2,1)} %bitcast.266), channel_id=1, replica_groups=mesh['seq'=4,'fsdp'=8] {'fsdp'}, dimensions={0}, use_global_device_ids=true | all-gather | bytes 2304 | tf_op jit(solution)/shard_map/all_gather | solution.py:179
  27.4 87.9 %all-gather.7.cloned.1.call-done = bf16[1024,3072]{1,0:T(8,128)(2,1)} async-done(((bf16[128,3072]{1,0:T(8,128)(2,1)}), bf16[1024,3072]{1,0:T(8,128)(2,1)}) %all-gather.7.cloned.1.call-update) | async-done | bytes 6291472 | tf_op jit(solution)/shard_map/all_gather | solution.py:177
  115.3 8.6 copy.74
  136.5 7.8 maximum_select_fusion.2
  144.3 8.3 collective-permute-start.2
  162.3 15.6 %while.27 = (s32[]{:T(128)}, bf16[2,512,4,64]{1,3,2,0:T(8,128)(2,1)S(1)}, f32[2,4,512]{2,1,0:T(4,128)S(1)}, s32[2,512]{1,0:T(2,128)S(1)}, s32[1,1024]{1,0:T(1,12...) while((s32[]{:T(128)}, ...), condition=%wide.region_5.6_spmd, body=%wide.region_2.5_spmd.sunk | while | flops 564132864 | bytes 29186172 | solution.py:91
  194.6 104.0 %all-gather.1 = bf16[8,1,128]{2,1,0:T(2,128)(2,1)S(1)} all-gather(bf16[1,1,128]{2,1,0:T(2,128)(2,1)S(1)} %bitcast.267), channel_id=1, replica_groups=mesh['seq'=4,'fsdp'=8] {'fsdp'}, dimensions={0}, use_global_device_ids=true | all-gather | bytes 2304 | tf_op jit(solution)/shard_map/all_gather | solution.py:184
  308.2 204.5 %collective-permute-done.2 = bf16[512,5248]{1,0:T(8,128)(2,1)} collective-permute-done((bf16[512,5248]{1,0:T(8,128)(2,1)}, bf16[512,5248]{1,0:T(8,128)(2,1)}, u32[]{:S(2)}, u32[]{:S(2)}) %collective-permute-start.2) | collective-permute-done | bytes 5373984 | tf_op jit(solution)/shard_map/ppermute | solution.py:22
  512.7 10.9 fusion.45
  523.6 9.2 add_convert_fusion
  532.8 6.8 fusion.54
  549.1 7.0 fusion.74
  563.7 7.8 all-to-all-done.2
  576.3 42.3 %while.28 = (s32[]{:T(128)}, f32[1024,4,64]{0,2,1:T(8,128)S(1)}, f32[1024,4,64]{0,2,1:T(8,128)}, bf16[2,512,4,64]{1,3,2,0:T(8,128)(2,1)}, bf16[2,512,4,64]{1,3,2...) while((s32[]{:T(128)}, f32[1024,4,64]{0,2,1:T(8,128)S(1)}, ...), condition=%wide.region_12.13_spmd.clone, body=%wide.region_10.12_spmd.clone.sunk | while | flops 1377172480 | bytes 143735600 | solution.py:149
  626.2 27.5 %all_to_all.54 = bf16[1024,3,1,256]{3,1,2,0:T(4,128)(2,1)S(1)} all-to-all(bf16[1024,3,1,256]{3,1,2,0:T(4,128)(2,1)S(1)} %copy.90), channel_id=1, replica_groups=mesh['seq'=4,'fsdp'=8] {'seq'}, dimensions={0} | all-to-all | bytes 3145728 | tf_op jit(solution)/shard_map/all_to_all | solution.py:300
  661.2 6.5 fusion.78
  669.0 11.0 fusion.53
  680.2 42.1 %reduce-scatter.11.cloned.1.call-done = f32[328,1024]{1,0:T(8,128)} async-done(((f32[2624,1024]{1,0:T(8,128)}), f32[328,1024]{1,0:T(8,128)}) %reduce-scatter.11.cloned.1.call-update) | async-done | bytes 1343504 | tf_op jit(solution)/shard_map/reduce_scatter | solution.py:273
  722.3 129.9 %reduce-scatter.5.cloned.1.call-done = f32[128,3072]{1,0:T(8,128)} async-done(((f32[1024,3072]{1,0:T(8,128)}), f32[128,3072]{1,0:T(8,128)}) %reduce-scatter.5.cloned.1.call-update) | async-done | bytes 1572880 | tf_op jit(solution)/shard_map/reduce_scatter | solution.py:321
  852.2 213.4 %reduce-scatter.9.cloned.1.call-done = f32[128,5248]{1,0:T(8,128)} async-done(((f32[1024,5248]{1,0:T(8,128)}), f32[128,5248]{1,0:T(8,128)}) %reduce-scatter.9.cloned.1.call-update) | async-done | bytes 2686992 | tf_op jit(solution)/shard_map/reduce_scatter | solution.py:272
  1066.9 39.2 %all-reduce.8 = (f32[1]{0:T(128)}, f32[1]{0:T(128)}, f32[1]{0:T(128)}, f32[]{:T(128)}) all-reduce(f32[1]{0:T(128)} %bitcast.50, f32[1]{0:T(128)} %bitcast.49, f32[1]{0:T(128)} %bitcast.48, f32[]{:T(128)} %get-tuple-element.337), channel_id=1, replica_groups=mesh['seq'=4,'fsdp'=8] {'seq','fsdp'}, use_global_device_ids=true, to_apply=%region_34.35 | all-reduce | flops 4 | bytes 32 | tf_op jit(solution)/shard_map/psum | solution.py:228
  1115.8 16.0 %all-reduce.9 = (f32[1024]{0:T(1024)S(1)}, f32[1024]{0:T(1024)S(1)}) all-reduce(f32[1024]{0:T(1024)S(1)} %get-tuple-element.272, f32[1024]{0:T(1024)S(1)} %copy-done.36), channel_id=6, replica_groups=mesh['seq'=4,'fsdp'=8] {'fsdp'}, use_global_device_ids=true, to_apply=%region_24.25.clone | all-reduce | flops 2048 | bytes 16384
  1131.9 9.2 all-reduce.10
  1144.0 60.8 %all-reduce.14.cloned.1.call-done = (f32[128,3072]{1,0:T(8,128)}, f32[128,1024]{1,0:T(8,128)}, f32[128,5248]{1,0:T(8,128)}, f32[328,1024]{1,0:T(8,128)}) async-done(((f32[128,3072]{1,0:T(8,128)}, f32[128,1024]{1,0:T(8,128)}, f32[128,5248]{1,0:T(8,128)}, f32[328,1024]{1,0:T(8,128)}), (f32[128,3072]{1,0:T(8,128)}, f32[128,1024]{1,0:T(8,128)}, f32[128,5248]{1,0:T(8,128)}, ...) | async-done | bytes 6127632 | tf_op jit(solution)/shard_map/psum | solution.py:325
  (236 shorter events, 171.0 us)
Async XLA Ops:
  7.2 108.1 %all-gather.7.cloned.1.call-start = ((), (), s32[]{:S(2)}) async-start(), calls=%async_computation.8 | async-start | bytes 7077888 | tf_op jit(solution)/shard_map/all_gather | solution.py:177
  7.9 296.5 %all-gather.9.cloned.1.call-start = ((), (), s32[]{:S(2)}) async-start(), calls=%async_computation.9 | async-start | bytes 2359296 | tf_op jit(solution)/shard_map/all_gather | solution.py:178
  8.7 514.9 %all-gather.11.cloned.1.call-start = ((), (), s32[]{:S(2)}) async-start(), calls=%async_computation.10 | async-start | bytes 6045696 | tf_op jit(solution)/shard_map/all_gather | solution.py:183
  9.4 523.4 %all-gather.13.cloned.1.call-start = ((), (), s32[]{:S(2)}) async-start(), calls=%async_computation.11 | async-start | bytes 12091392 | tf_op jit(solution)/shard_map/all_gather | solution.py:245
  10.0 14.9 %collective-permute-start = (bf16[128,5248]{1,0:T(8,128)(2,1)}, bf16[128,5248]{1,0:T(8,128)(2,1)S(1)}, u32[]{:S(2)}, u32[]{:S(2)}) collective-permute-start(bf16[128,5248]{1,0:T(8,128)(2,1)} %param.19), channel_id=1, source_target_pairs={{0,1},{1,0},{2,3},{3,2},{4,5},{5,4},{6,7},{7,6},{8,9},{9,8},{10,11... | collective-permute-start | bytes 4030472 | tf_op jit(solution)/shard_map/ppermute | solution.py:22
  23.7 100.3 %copy-start.26 = (f32[8,1,128]{2,1,0:T(1,128)}, f32[8,1,128]{2,1,0:T(1,128)S(1)}, u32[]{:S(2)}) copy-start(f32[8,1,128]{2,1,0:T(1,128)S(1)} %convert_element_type.149) | copy-start | bytes 12292
  26.8 109.7 %collective-permute-start.1 = (bf16[256,5248]{1,0:T(8,128)(2,1)}, bf16[256,5248]{1,0:T(8,128)(2,1)}, u32[]{:S(2)}, u32[]{:S(2)}) collective-permute-start(bf16[256,5248]{1,0:T(8,128)(2,1)} %maximum_select_fusion.3), channel_id=1, source_target_pairs={{0,2},{1,3},{2,0},{3,1},{4,6},{5,7},{6,4},{7,5},{8,10},{9,11},{10,... | collective-permute-start | bytes 8060936 | tf_op jit(solution)/shard_map/ppermute | solution.py:22
  26.9 97.1 %copy-start.28 = (f32[256]{0:T(256)}, f32[256]{0:T(256)S(1)}, u32[]{:S(2)}) copy-start(f32[256]{0:T(256)S(1)} %broadcast_multiply_fusion.1) | copy-start | bytes 3076
  27.2 96.8 %copy-start.34 = (f32[256]{0:T(256)}, f32[256]{0:T(256)S(1)}, u32[]{:S(2)}) copy-start(f32[256]{0:T(256)S(1)} %fusion.61) | copy-start | bytes 3076
  27.2 96.8 %copy-start.30 = (f32[256]{0:T(256)}, f32[256]{0:T(256)S(1)}, u32[]{:S(2)}) copy-start(f32[256]{0:T(256)S(1)} %fusion.80) | copy-start | bytes 3076
  27.4 101.7 %copy-start.22 = (f32[256,32]{0,1:T(8,128)}, f32[256,32]{0,1:T(8,128)S(1)}, u32[]{:S(2)}) copy-start(f32[256,32]{0,1:T(8,128)S(1)} %get-tuple-element.374) | copy-start | bytes 98308
  27.4 101.7 %copy-start.24 = (f32[256,32]{0,1:T(8,128)}, f32[256,32]{0,1:T(8,128)S(1)}, u32[]{:S(2)}) copy-start(f32[256,32]{0,1:T(8,128)S(1)} %get-tuple-element.375) | copy-start | bytes 98308
  130.9 23.0 %all-to-all-start = ((bf16[256,3,4,256]{0,3,1,2:T(8,128)(2,1)}), bf16[256,3,4,256]{0,3,1,2:T(8,128)(2,1)S(1)}, u32[]{:S(2)}, u32[]{:S(2)}) async-start(bf16[256,3,4,256]{0,3,1,2:T(8,128)(2,1)} %pad_maximum_fusion.3), calls=%async_computation | async-start | bytes 3145728 | tf_op jit(solution)/shard_map/all_to_all | solution.py:203
  144.3 368.4 %collective-permute-start.2 = (bf16[512,5248]{1,0:T(8,128)(2,1)}, bf16[512,5248]{1,0:T(8,128)(2,1)}, u32[]{:S(2)}, u32[]{:S(2)}) collective-permute-start(bf16[512,5248]{1,0:T(8,128)(2,1)} %maximum_select_fusion.2), channel_id=1, source_target_pairs={{0,4},{1,5},{2,6},{3,7},{4,0},{5,1},{6,2},{7,3},{8,12},{9,13},{10,... | collective-permute-start | bytes 16121864 | tf_op jit(solution)/shard_map/ppermute | solution.py:22
  190.4 108.9 %all-to-all-start.1 = ((bf16[4,2,32768]{2,1,0:T(2,128)(2,1)}), bf16[4,2,32768]{2,1,0:T(2,128)(2,1)}, u32[]{:S(2)}, u32[]{:S(2)}) async-start(bf16[4,2,32768]{2,1,0:T(2,128)(2,1)} %reshape.507), calls=%async_computation.1 | async-start | bytes 1048576 | tf_op jit(solution)/shard_map/all_to_all | solution.py:216
  194.5 485.6 %reduce-scatter.7.cloned.1.call-start = ((), (), s32[]{:S(2)}) async-start(), calls=%async_computation.13 | async-start | bytes 4718592 | tf_op jit(solution)/shard_map/reduce_scatter | solution.py:322
  307.9 235.7 %copy-start.4 = (f32[256,1024]{1,0:T(8,128)}, f32[256,1024]{1,0:T(8,128)S(1)}, u32[]{:S(2)}) copy-start(f32[256,1024]{1,0:T(8,128)S(1)} %get-tuple-element.342) | copy-start | bytes 3145732
  548.1 174.2 %reduce-scatter.11.cloned.1.call-start = ((), (), s32[]{:S(2)}) async-start(), calls=%async_computation.15 | async-start | bytes 12091392 | tf_op jit(solution)/shard_map/reduce_scatter | solution.py:273
  559.4 12.1 all-to-all-start.2
  563.2 288.9 %reduce-scatter.5.cloned.1.call-start = ((), (), s32[]{:S(2)}) async-start(), calls=%async_computation.12 | async-start | bytes 14155776 | tf_op jit(solution)/shard_map/reduce_scatter | solution.py:321
  667.8 397.8 %reduce-scatter.9.cloned.1.call-start = ((), (), s32[]{:S(2)}) async-start(), calls=%async_computation.14 | async-start | bytes 24182784 | tf_op jit(solution)/shard_map/reduce_scatter | solution.py:272
  680.1 385.5 %copy-start.39 = (u32[32]{0:T(128)S(1)}, u32[32]{0:T(128)}, u32[]{:S(2)}) copy-start(u32[32]{0:T(128)} %constant.122) | copy-start | bytes 388
  680.1 524.7 %all-reduce.14.cloned.1.call-start = ((), (), s32[]{:S(2)}) async-start(), calls=%async_computation.16 | async-start | bytes 12255232 | tf_op jit(solution)/shard_map/psum | solution.py:325
  1109.2 31.9 %copy-start.33 = (f32[256]{0:T(256)S(1)}, f32[256]{0:T(256)}, u32[]{:S(2)}) copy-start(f32[256]{0:T(256)} %copy-done.32) | copy-start | bytes 3076
  (35 other events, 211.9 us)
Sparse Core Ops, SparseCore 0:
  9.6 105.6 all-gather.6
  116.9 35.3 all-gather.8
  154.0 179.7 all-gather.10
  335.3 147.8 all-gather.12
  548.2 61.5 reduce-scatter.6
  611.9 110.2 reduce-scatter.10
  724.6 127.5 reduce-scatter.4
  854.5 210.9 reduce-scatter.8
  1069.5 135.2 all-reduce.13
